TPU v7x, 512 devices: a whole 4x4x16 slice. The times are simulated.
512 devices in a mesh: shot: 4 (over x), gx: 16 (over z_hi, y), gy: 8 (over z_lo, core).
Axes of the slice: x: 4, y: 4, z: 16 (z_hi: 4, z_lo: 4; z = z_hi * 4 + z_lo), core: 2. Of those that a mesh axis runs over, the one named last changes fastest.
Arguments:
- forward_now: float32 [4, 512, 256, 128], P('shot', 'gx', 'gy'), may hold values from -3 to 3
- forward_later: float32 [4, 512, 256, 128], P('shot', 'gx', 'gy'), may hold values from -3 to 3
- adjoint_now: float32 [4, 512, 256, 128], P('shot', 'gx', 'gy'), may hold values from -3 to 3
- adjoint_later: float32 [4, 512, 256, 128], P('shot', 'gx', 'gy'), may hold values from -3 to 3
- courant: float32 [512, 256, 128], P('gx', 'gy'), may hold values from 0.15 to 0.45
- source_cells: int32 [4, 16, 3], P('shot'), may hold values from 0 to 511, as said below
- source_wave: float32 [4, 3, 16], P('shot'), may hold values from -6 to 6
- receiver_cells: int32 [4, 4096, 3], P('shot'), may hold values from 0 to 511, as said below
- residual: float32 [4, 3, 4096], P('shot'), may hold values from -6 to 6
Outputs:
- forward_first: float32 [4, 512, 256, 128], P('shot', 'gx', 'gy')
- adjoint_first: float32 [4, 512, 256, 128], P('shot', 'gx', 'gy')
- gradient: float32 [512, 256, 128], P('gx', 'gy')
Inputs may be any that keep to these rules, and one draw needn't show every extreme that they name: `source_cells`: entry [s, i] holds the first, second and depth cell index of source i of shot group s, each inside the grid of 512 x 256 x 128 cells; cells may repeat. `receiver_cells`: entry [s, r] holds the first, second and depth cell index of receiver r of shot group s, each inside the grid of 512 x 256 x 128 cells; cells may repeat.
All inputs are finite; a program needn't handle non-finite values.
Results may differ from a plain program's by a relative error of at most 0.0003.
Values sent between devices are 32-bit elements; how exact they have to be, the bound alone decides.
A program may use at most 64 MiB of HBM per device.

v0:
```python
import math
import jax
import jax.numpy as jnp
from jax import lax
from jax.sharding import PartitionSpec as P

STEPS = 3
COEFFS = (-205.0 / 72.0, 8.0 / 5.0, -1.0 / 5.0, 8.0 / 315.0, -1.0 / 560.0)
GRAD_SCALE = 0.1


def extended_2(block, sides, width):
    for axis, dim in sides:
        count = lax.axis_size(axis)
        forward = [(i, i + 1) for i in range(count - 1)]
        backward = [(target, source) for source, target in forward]
        low = lax.ppermute(
            lax.slice_in_dim(block, block.shape[dim] - width, None, axis=dim), axis, forward
        )
        high = lax.ppermute(lax.slice_in_dim(block, 0, width, axis=dim), axis, backward)
        block = jnp.concatenate([low, block, high], axis=dim)
    return block


def stencil(extended):
    full = jnp.pad(extended, [(0, 0)] * (extended.ndim - 1) + [(4, 4)])
    rows_x = extended.shape[-3] - 8
    rows_y = extended.shape[-2] - 8
    depth = extended.shape[-1]

    def shifted(step_x, step_y, step_z):
        return full[
            ...,
            4 + step_x : 4 + step_x + rows_x,
            4 + step_y : 4 + step_y + rows_y,
            4 + step_z : 4 + step_z + depth,
        ]

    summed = 3.0 * COEFFS[0] * shifted(0, 0, 0)
    for reach in range(1, 5):
        pairs = (
            shifted(reach, 0, 0)
            + shifted(-reach, 0, 0)
            + (shifted(0, reach, 0) + shifted(0, -reach, 0))
        )
        pairs = pairs + (shifted(0, 0, reach) + shifted(0, 0, -reach))
        summed = summed + COEFFS[reach] * pairs
    return summed


def inject(stacked, which, cells, values, start_x, start_y):
    extent_x = stacked.shape[1]
    extent_y = stacked.shape[2]
    depth = stacked.shape[3]
    count = cells.shape[0]
    block = math.gcd(count, 512)
    blocks = count // block
    cell_blocks = cells.reshape(blocks, block, 3)
    value_blocks = values.reshape(blocks, block)
    range_x = jnp.arange(extent_x, dtype=jnp.int32)
    range_y = jnp.arange(extent_y, dtype=jnp.int32)
    range_z = jnp.arange(depth, dtype=jnp.int32)

    def one_block(total, items):
        chosen, amounts = items
        hit_x = jnp.where(chosen[:, 0:1] - start_x == range_x[None, :], amounts[:, None], 0.0)
        hit_y = (chosen[:, 1:2] - start_y == range_y[None, :]).astype(jnp.float32)
        hit_z = (chosen[:, 2:3] == range_z[None, :]).astype(jnp.float32)
        plane = (hit_x[:, :, None] * hit_y[:, None, :]).reshape(block, extent_x * extent_y)
        added = lax.dot_general(
            plane,
            hit_z,
            (((0,), (0,)), ((), ())),
            precision=lax.Precision.HIGHEST,
            preferred_element_type=jnp.float32,
        )
        return (total + added, None)

    start = jnp.zeros((extent_x * extent_y, depth), jnp.float32)
    total, unused = lax.scan(one_block, start, (cell_blocks, value_blocks))
    return stacked.at[which].add(total.reshape(extent_x, extent_y, depth))


def add_term(summed, term):
    return summed + term


def shards(
    forward_now,
    forward_later,
    adjoint_now,
    adjoint_later,
    courant,
    source_cells,
    source_wave,
    receiver_cells,
    residual,
):
    rows_x = courant.shape[0]
    rows_y = courant.shape[1]
    anchor_x = lax.axis_index("gx") * rows_x
    anchor_y = lax.axis_index("gy") * rows_y
    sources = source_cells[0]
    amplitude = source_wave[0]
    receivers = receiver_cells[0]
    misfit = residual[0]
    summed = jnp.zeros(courant.shape, jnp.float32)
    current = jnp.concatenate([forward_now, adjoint_now], 0)
    later = jnp.concatenate([forward_later, adjoint_later], 0)
    squared = courant * courant
    for step in range(STEPS):
        extended = extended_2(current, (("gx", 1), ("gy", 2)), 4)
        curved = stencil(extended)
        term = 2.0 * courant * current[1] * curved[0]
        summed = add_term(summed, term)
        earlier = 2.0 * current - later + squared * curved
        earlier = inject(earlier, 0, sources, amplitude[step], anchor_x, anchor_y)
        earlier = inject(earlier, 1, receivers, misfit[step], anchor_x, anchor_y)
        later = current
        current = earlier
    gradient = lax.psum(summed, "shot")
    return (current[0:1], current[1:2], GRAD_SCALE * gradient)


def solution(mesh):
    placed = (
        P("shot", "gx", "gy", None),
        P("shot", "gx", "gy", None),
        P("shot", "gx", "gy", None),
        P("shot", "gx", "gy", None),
        P("gx", "gy", None),
        P("shot", None, None),
        P("shot", None, None),
        P("shot", None, None),
        P("shot", None, None),
    )
    return jax.shard_map(
        shards,
        mesh=mesh,
        in_specs=placed,
        out_specs=(P("shot", "gx", "gy", None), P("shot", "gx", "gy", None), P("gx", "gy", None)),
        check_vma=False,
    )
```

profile of v0, /device:TPU:8, one launch (start us, length us, event | category | flops | bytes accessed | tf_op | source)
XLA Modules:
  0.0 263.9 jit_solution(13298024963650580862)
XLA Ops:
  10.3 7.7 %collective-permute-start = (f32[2,4,32,128]{3,2,1,0:T(8,128)}, f32[2,4,32,128]{3,2,1,0:T(8,128)S(1)}, u32[]{:S(2)}, u32[]{:S(2)}) collective-permute-start(f32[2,4,32,128]{3,2,1,0:T(8,128)} %get-tuple-element.641), channel_id=1, source_target_pairs={{8,0},{16,8},{24,16},{32,24},{40,32},{48,40},{56,48},{64,56},{72,6... | collective-permute-start | bytes 393224 | tf_op jit(solution)/shard_map/ppermute | solution.py:20
  18.0 1.9 collective-permute-start.1
  22.3 25.7 %while.60 = (s32[]{:T(128)}, f32[1024,128]{1,0:T(8,128)}, s32[8,512,3]{1,2,0:T(4,128)S(1)}, s32[]{:T(128)}, f32[8,512]{1,0:T(8,128)S(1)}, /*index=5*/s32[]{:T(128)}, s32[]{:T(128)}, s32[]{:T(128)}) while((s32[]{:T(128)}, f32[1024,128]{1,0:T(8,128)}, s32[8,512,3]{1,2,0:T(4,128)S(1)}, s32[]{:T(128)}, ...), condition=%wide.region_1.2_spmd.clone.clone, body=%wide.region_0.1_spmd.clone.clone.sunk | while | flops 806224896 | bytes 5541999 | solution.py:80
  22.6 2.0 convolution_add_fusion.6
  24.9 3.0 %convolution_add_fusion.6 = f32[1024,128]{1,0:T(8,128)} fusion(f32[512,1024]{0,1:T(8,128)S(1)} %bitcast.147, f32[1024,128]{1,0:T(8,128)} %get-tuple-element.792, pred[]{:T(512)S(6)} %compare.91, s32[512]{0:T(512)S(1)} %bitcast.159), kind=kOutput, calls=%fused_computation.6.clone.1 | convolution fusion | flops 805634048 | bytes 3147777 | tf_op jit(solution)/shard_map/while/body/eval_jaxpr/dot_general | solution.py:70
  28.3 3.0 %convolution_add_fusion.6 = f32[1024,128]{1,0:T(8,128)} fusion(f32[512,1024]{0,1:T(8,128)S(1)} %bitcast.147, f32[1024,128]{1,0:T(8,128)} %get-tuple-element.792, pred[]{:T(512)S(6)} %compare.91, s32[512]{0:T(512)S(1)} %bitcast.159), kind=kOutput, calls=%fused_computation.6.clone.1 | convolution fusion | flops 805634048 | bytes 3147777 | tf_op jit(solution)/shard_map/while/body/eval_jaxpr/dot_general | solution.py:70
  31.6 3.0 %convolution_add_fusion.6 = f32[1024,128]{1,0:T(8,128)} fusion(f32[512,1024]{0,1:T(8,128)S(1)} %bitcast.147, f32[1024,128]{1,0:T(8,128)} %get-tuple-element.792, pred[]{:T(512)S(6)} %compare.91, s32[512]{0:T(512)S(1)} %bitcast.159), kind=kOutput, calls=%fused_computation.6.clone.1 | convolution fusion | flops 805634048 | bytes 3147777 | tf_op jit(solution)/shard_map/while/body/eval_jaxpr/dot_general | solution.py:70
  34.9 3.0 %convolution_add_fusion.6 = f32[1024,128]{1,0:T(8,128)} fusion(f32[512,1024]{0,1:T(8,128)S(1)} %bitcast.147, f32[1024,128]{1,0:T(8,128)} %get-tuple-element.792, pred[]{:T(512)S(6)} %compare.91, s32[512]{0:T(512)S(1)} %bitcast.159), kind=kOutput, calls=%fused_computation.6.clone.1 | convolution fusion | flops 805634048 | bytes 3147777 | tf_op jit(solution)/shard_map/while/body/eval_jaxpr/dot_general | solution.py:70
  38.3 3.0 %convolution_add_fusion.6 = f32[1024,128]{1,0:T(8,128)} fusion(f32[512,1024]{0,1:T(8,128)S(1)} %bitcast.147, f32[1024,128]{1,0:T(8,128)} %get-tuple-element.792, pred[]{:T(512)S(6)} %compare.91, s32[512]{0:T(512)S(1)} %bitcast.159), kind=kOutput, calls=%fused_computation.6.clone.1 | convolution fusion | flops 805634048 | bytes 3147777 | tf_op jit(solution)/shard_map/while/body/eval_jaxpr/dot_general | solution.py:70
  41.6 3.0 %convolution_add_fusion.6 = f32[1024,128]{1,0:T(8,128)} fusion(f32[512,1024]{0,1:T(8,128)S(1)} %bitcast.147, f32[1024,128]{1,0:T(8,128)} %get-tuple-element.792, pred[]{:T(512)S(6)} %compare.91, s32[512]{0:T(512)S(1)} %bitcast.159), kind=kOutput, calls=%fused_computation.6.clone.1 | convolution fusion | flops 805634048 | bytes 3147777 | tf_op jit(solution)/shard_map/while/body/eval_jaxpr/dot_general | solution.py:70
  45.0 3.0 %convolution_add_fusion.6 = f32[1024,128]{1,0:T(8,128)} fusion(f32[512,1024]{0,1:T(8,128)S(1)} %bitcast.147, f32[1024,128]{1,0:T(8,128)} %get-tuple-element.792, pred[]{:T(512)S(6)} %compare.91, s32[512]{0:T(512)S(1)} %bitcast.159), kind=kOutput, calls=%fused_computation.6.clone.1 | convolution fusion | flops 805634048 | bytes 3147777 | tf_op jit(solution)/shard_map/while/body/eval_jaxpr/dot_general | solution.py:70
  49.5 3.0 %collective-permute-start.3 = (f32[2,40,4,128]{3,2,1,0:T(4,128)S(1)}, f32[2,40,4,128]{3,2,1,0:T(4,128)S(1)}, u32[]{:S(2)}, u32[]{:S(2)}) collective-permute-start(f32[2,40,4,128]{3,2,1,0:T(4,128)S(1)} %get-tuple-element.634), channel_id=1, source_target_pairs={{0,1},{1,2},{2,3},{3,4},{4,5},{5,6},{6,7},{8,9},{9,10},{10,11},{11... | collective-permute-start | bytes 491528 | tf_op jit(solution)/shard_map/ppermute | solution.py:17
  55.9 1.5 pad_maximum_fusion
  57.4 3.1 %select_maximum_fusion.8 = f32[2,40,40,136]{3,2,1,0:T(8,128)S(1)} fusion(f32[2,40,4,128]{3,2,1,0:T(4,128)} %copy-done.14, f32[2,40,4,128]{3,2,1,0:T(4,128)} %copy-done.15, f32[2,4,32,128]{3,2,1,0:T(8,128)S(1)} %collective-permute-done, f32[2,32,32,128]{3,2,1,0:T(8,128)S(1)} %constant_dynamic-update-slice_fusion, f32[2,4,32,128]{3,2,1,0:T(8,128)S(1)} %collective-permute-done.1), kind=kLoop, calls=%fused_computation.52 | loop fusion | flops 5222400 | bytes 3379200 | tf_op jit(solution)/shard_map/concatenate | solution.py:21
  60.5 6.2 %fusion.105 = (f32[2,32,32,128]{3,2,1,0:T(8,128)S(1)}, f32[2,32,32,128]{3,2,1,0:T(8,128)}) fusion(f32[1,32,32,128]{3,2,1,0:T(8,128)} %param.30, f32[1,32,32,128]{3,2,1,0:T(8,128)} %param.28, f32[2,32,32,128]{3,2,1,0:T(8,128)S(1)} %constant_dynamic-update-slice_fusion, f32[32,32,128]{2,1,0:T(8,128)S(1)} %copy-done.6, ...), kind=kLoop, calls=%fused_computation.216 | loop fusion | flops 11010048 | bytes 21757952 | tf_op jit(solution)/shard_map/add | solution.py:116
  68.5 3.9 %collective-permute-start.4 = (f32[2,4,32,128]{3,2,1,0:T(8,128)S(1)}, f32[2,4,32,128]{3,2,1,0:T(8,128)S(1)}, u32[]{:S(2)}, u32[]{:S(2)}) collective-permute-start(f32[2,4,32,128]{3,2,1,0:T(8,128)S(1)} %get-tuple-element.639), channel_id=1, source_target_pairs={{8,0},{16,8},{24,16},{32,24},{40,32},{48,40},{56,48},{64,56},{72,6... | collective-permute-start | bytes 393224 | tf_op jit(solution)/shard_map/ppermute | solution.py:20
  72.4 1.9 collective-permute-start.5
  74.4 1.4 collective-permute-done.4
  75.8 3.7 %collective-permute-done.5 = f32[2,4,32,128]{3,2,1,0:T(8,128)S(1)} collective-permute-done((f32[2,4,32,128]{3,2,1,0:T(8,128)S(1)}, f32[2,4,32,128]{3,2,1,0:T(8,128)S(1)}, u32[]{:S(2)}, u32[]{:S(2)}) %collective-permute-start.5) | collective-permute-done | bytes 131104 | tf_op jit(solution)/shard_map/ppermute | solution.py:17
  81.5 3.7 %collective-permute-start.7 = (f32[2,40,4,128]{3,2,1,0:T(4,128)}, f32[2,40,4,128]{3,2,1,0:T(4,128)}, u32[]{:S(2)}, u32[]{:S(2)}) collective-permute-start(f32[2,40,4,128]{3,2,1,0:T(4,128)} %get-tuple-element.630), channel_id=1, source_target_pairs={{0,1},{1,2},{2,3},{3,4},{4,5},{5,6},{6,7},{8,9},{9,10},{10,11},{11... | collective-permute-start | bytes 491528 | tf_op jit(solution)/shard_map/ppermute | solution.py:17
  85.2 25.7 %while.61 = (s32[]{:T(128)}, f32[1024,128]{1,0:T(8,128)}, s32[8,512,3]{1,2,0:T(4,128)S(1)}, s32[]{:T(128)}, f32[8,512]{1,0:T(8,128)S(1)}, /*index=5*/s32[]{:T(128)}, s32[]{:T(128)}, s32[]{:T(128)}) while((s32[]{:T(128)}, f32[1024,128]{1,0:T(8,128)}, s32[8,512,3]{1,2,0:T(4,128)S(1)}, s32[]{:T(128)}, ...), condition=%wide.region_3.4_spmd.clone.clone, body=%wide.region_2.3_spmd.clone.clone.sunk | while | flops 806224896 | bytes 5541999 | solution.py:80
  85.5 2.0 convolution_add_fusion.7
  87.8 3.0 %convolution_add_fusion.7 = f32[1024,128]{1,0:T(8,128)} fusion(f32[512,1024]{0,1:T(8,128)S(1)} %bitcast.148, f32[1024,128]{1,0:T(8,128)} %get-tuple-element.816, pred[]{:T(512)S(6)} %compare.92, s32[512]{0:T(512)S(1)} %bitcast.160), kind=kOutput, calls=%fused_computation.18.clone.1 | convolution fusion | flops 805634048 | bytes 3147777 | tf_op jit(solution)/shard_map/while/body/eval_jaxpr/dot_general | solution.py:70
  91.2 3.0 %convolution_add_fusion.7 = f32[1024,128]{1,0:T(8,128)} fusion(f32[512,1024]{0,1:T(8,128)S(1)} %bitcast.148, f32[1024,128]{1,0:T(8,128)} %get-tuple-element.816, pred[]{:T(512)S(6)} %compare.92, s32[512]{0:T(512)S(1)} %bitcast.160), kind=kOutput, calls=%fused_computation.18.clone.1 | convolution fusion | flops 805634048 | bytes 3147777 | tf_op jit(solution)/shard_map/while/body/eval_jaxpr/dot_general | solution.py:70
  94.5 3.0 %convolution_add_fusion.7 = f32[1024,128]{1,0:T(8,128)} fusion(f32[512,1024]{0,1:T(8,128)S(1)} %bitcast.148, f32[1024,128]{1,0:T(8,128)} %get-tuple-element.816, pred[]{:T(512)S(6)} %compare.92, s32[512]{0:T(512)S(1)} %bitcast.160), kind=kOutput, calls=%fused_computation.18.clone.1 | convolution fusion | flops 805634048 | bytes 3147777 | tf_op jit(solution)/shard_map/while/body/eval_jaxpr/dot_general | solution.py:70
  97.9 3.0 %convolution_add_fusion.7 = f32[1024,128]{1,0:T(8,128)} fusion(f32[512,1024]{0,1:T(8,128)S(1)} %bitcast.148, f32[1024,128]{1,0:T(8,128)} %get-tuple-element.816, pred[]{:T(512)S(6)} %compare.92, s32[512]{0:T(512)S(1)} %bitcast.160), kind=kOutput, calls=%fused_computation.18.clone.1 | convolution fusion | flops 805634048 | bytes 3147777 | tf_op jit(solution)/shard_map/while/body/eval_jaxpr/dot_general | solution.py:70
  101.2 3.0 %convolution_add_fusion.7 = f32[1024,128]{1,0:T(8,128)} fusion(f32[512,1024]{0,1:T(8,128)S(1)} %bitcast.148, f32[1024,128]{1,0:T(8,128)} %get-tuple-element.816, pred[]{:T(512)S(6)} %compare.92, s32[512]{0:T(512)S(1)} %bitcast.160), kind=kOutput, calls=%fused_computation.18.clone.1 | convolution fusion | flops 805634048 | bytes 3147777 | tf_op jit(solution)/shard_map/while/body/eval_jaxpr/dot_general | solution.py:70
  104.5 3.0 %convolution_add_fusion.7 = f32[1024,128]{1,0:T(8,128)} fusion(f32[512,1024]{0,1:T(8,128)S(1)} %bitcast.148, f32[1024,128]{1,0:T(8,128)} %get-tuple-element.816, pred[]{:T(512)S(6)} %compare.92, s32[512]{0:T(512)S(1)} %bitcast.160), kind=kOutput, calls=%fused_computation.18.clone.1 | convolution fusion | flops 805634048 | bytes 3147777 | tf_op jit(solution)/shard_map/while/body/eval_jaxpr/dot_general | solution.py:70
  107.9 3.0 %convolution_add_fusion.7 = f32[1024,128]{1,0:T(8,128)} fusion(f32[512,1024]{0,1:T(8,128)S(1)} %bitcast.148, f32[1024,128]{1,0:T(8,128)} %get-tuple-element.816, pred[]{:T(512)S(6)} %compare.92, s32[512]{0:T(512)S(1)} %bitcast.160), kind=kOutput, calls=%fused_computation.18.clone.1 | convolution fusion | flops 805634048 | bytes 3147777 | tf_op jit(solution)/shard_map/while/body/eval_jaxpr/dot_general | solution.py:70
  112.8 2.5 pad_maximum_fusion.1
  115.3 3.2 %select_maximum_fusion.4 = f32[2,40,40,136]{3,2,1,0:T(8,128)S(1)} fusion(f32[2,40,4,128]{3,2,1,0:T(4,128)} %collective-permute-done.6, f32[2,40,4,128]{3,2,1,0:T(4,128)} %collective-permute-done.7, f32[2,4,32,128]{3,2,1,0:T(8,128)S(1)} %collective-permute-done.4, f32[2,32,32,128]{3,2,1,0:T(8,128)S(1)} %fusion.114, ...), kind=kLoop, calls=%fused_computation.48 | loop fusion | flops 5222400 | bytes 3379200 | tf_op jit(solution)/shard_map/concatenate | solution.py:21
  118.5 6.3 %multiply_add_fusion.1 = (f32[2,32,32,128]{3,2,1,0:T(8,128)}, f32[2,32,32,128]{3,2,1,0:T(8,128)}) fusion(f32[2,32,32,128]{3,2,1,0:T(8,128)S(1)} %copy-done.1, f32[2,32,32,128]{3,2,1,0:T(8,128)S(1)} %fusion.114, f32[32,32,128]{2,1,0:T(8,128)S(1)} %copy-done.7, f32[2,40,40,136]{3,2,1,0:T(8,128)S(1)} %select_maximum_fusion.4, ...), kind=kLoop, calls=%fused_computation.218 | loop fusion | flops 10747904 | bytes 21757952 | tf_op jit(solution)/shard_map/add | solution.py:116
  124.8 2.6 fusion.25
  128.8 1.9 collective-permute-start.8
  130.7 3.9 %collective-permute-start.9 = (f32[2,4,32,128]{3,2,1,0:T(8,128)S(1)}, f32[2,4,32,128]{3,2,1,0:T(8,128)S(1)}, u32[]{:S(2)}, u32[]{:S(2)}) collective-permute-start(f32[2,4,32,128]{3,2,1,0:T(8,128)S(1)} %get-tuple-element.636), channel_id=1, source_target_pairs={{0,8},{8,16},{16,24},{24,32},{32,40},{40,48},{48,56},{56,64},{64,7... | collective-permute-start | bytes 393224 | tf_op jit(solution)/shard_map/ppermute | solution.py:17
  134.6 1.6 collective-permute-done.8
  136.2 2.7 %collective-permute-done.9 = f32[2,4,32,128]{3,2,1,0:T(8,128)S(1)} collective-permute-done((f32[2,4,32,128]{3,2,1,0:T(8,128)S(1)}, f32[2,4,32,128]{3,2,1,0:T(8,128)S(1)}, u32[]{:S(2)}, u32[]{:S(2)}) %collective-permute-start.9) | collective-permute-done | bytes 131104 | tf_op jit(solution)/shard_map/ppermute | solution.py:17
  141.0 3.7 %collective-permute-start.11 = (f32[2,40,4,128]{3,2,1,0:T(4,128)}, f32[2,40,4,128]{3,2,1,0:T(4,128)}, u32[]{:S(2)}, u32[]{:S(2)}) collective-permute-start(f32[2,40,4,128]{3,2,1,0:T(4,128)} %get-tuple-element.626), channel_id=1, source_target_pairs={{0,1},{1,2},{2,3},{3,4},{4,5},{5,6},{6,7},{8,9},{9,10},{10,11},{11... | collective-permute-start | bytes 491528 | tf_op jit(solution)/shard_map/ppermute | solution.py:17
  145.4 2.9 %pad_maximum_fusion.2 = (f32[2,40,36,128]{3,2,1,0:T(8,128)}, f32[2,40,36,128]{3,2,1,0:T(8,128)}) fusion(f32[2,40,4,128]{3,2,1,0:T(4,128)} %collective-permute-done.10, f32[2,4,32,128]{3,2,1,0:T(8,128)S(1)} %collective-permute-done.8, f32[2,32,32,128]{3,2,1,0:T(8,128)S(1)} %fusion.115, f32[2,4,32,128]{3,2,1,0:T(8,128)S(1)} %collective-permute-done.9, ...), kind=kLoop, calls=%fused_computation.79 | loop fusion | flops 2211840 | bytes 4587520 | tf_op jit(solution)/shard_map/concatenate | solution.py:21
  148.3 3.1 %select_maximum_fusion = f32[2,40,40,136]{3,2,1,0:T(8,128)S(1)} fusion(f32[2,40,4,128]{3,2,1,0:T(4,128)} %collective-permute-done.10, f32[2,40,4,128]{3,2,1,0:T(4,128)} %collective-permute-done.11, f32[2,4,32,128]{3,2,1,0:T(8,128)S(1)} %collective-permute-done.8, f32[2,32,32,128]{3,2,1,0:T(8,128)S(1)} %fusion.115, ...), kind=kLoop, calls=%fused_computation.44 | loop fusion | flops 5222400 | bytes 3379200 | tf_op jit(solution)/shard_map/concatenate | solution.py:21
  151.5 7.4 %multiply_add_fusion = (f32[2,32,32,128]{3,2,1,0:T(8,128)}, f32[2,32,32,128]{3,2,1,0:T(8,128)}) fusion(f32[2,32,32,128]{3,2,1,0:T(8,128)S(1)} %fusion.114, f32[2,32,32,128]{3,2,1,0:T(8,128)S(1)} %fusion.115, f32[32,32,128]{2,1,0:T(8,128)S(1)} %copy-done.8, f32[2,40,40,136]{3,2,1,0:T(8,128)S(1)} %select_maximum_fusion, ...), kind=kLoop, calls=%fused_computation.217 | loop fusion | flops 10747904 | bytes 21757952 | tf_op jit(solution)/shard_map/add | solution.py:116
  158.9 3.3 %fusion.107 = f32[32,32,128]{2,1,0:T(8,128)} fusion(f32[2,32,32,128]{3,2,1,0:T(8,128)} %get-tuple-element.610, f32[2,32,32,128]{3,2,1,0:T(8,128)} %get-tuple-element.612, f32[2,32,32,128]{3,2,1,0:T(8,128)} %get-tuple-element.614, f32[1,32,32,128]{3,2,1,0:T(8,128)} %param.29, f32[32,32,128]{2,1,0:T(8,128)} %param.31, f32[1,32,32,128]{3,2,1,0:T(8,128)S(1)} %bitcast.151, ...), kind=kLoop, calls=%fused_computation.221 | loop fusion | flops 1441792 | bytes 5242880 | tf_op jit(solution)/shard_map/add | solution.py:85
  162.3 14.0 %while.62 = (s32[]{:T(128)}, f32[1024,128]{1,0:T(8,128)S(1)}, s32[8,512,3]{1,2,0:T(4,128)S(1)}, s32[]{:T(128)}, f32[8,512]{1,0:T(8,128)S(1)}, /*index=5*/s32[]{:T(128)}, s32[]{:T(128)}, s32[]{:T(128)}) while((s32[]{:T(128)}, f32[1024,128]{1,0:T(8,128)S(1)}, s32[8,512,3]{1,2,0:T(4,128)S(1)}, s32[]{:T(128)}, ...), condition=%wide.region_5.6_spmd.clone.clone, body=%wide.region_4.5_spmd.clone.clone.sunk | while | flops 806224896 | bytes 5541999 | solution.py:80
  164.4 1.4 convolution_add_fusion.8
  173.1 1.4 convolution_add_fusion.8
  176.6 2.5 fusion.26
  180.0 75.2 %all-reduce.5.cloned.1.call-done = f32[32,32,128]{2,1,0:T(8,128)} async-done(((f32[32,32,128]{2,1,0:T(8,128)}), f32[32,32,128]{2,1,0:T(8,128)}) %all-reduce.5.cloned.1.call-update) | async-done | bytes 524304 | tf_op jit(solution)/shard_map/psum | solution.py:121
  255.2 1.9 broadcast_multiply_fusion.3
  (246 shorter events, 36.6 us)
Async XLA Ops:
  7.2 12.7 %copy-start.9 = (f32[32,32,128]{2,1,0:T(8,128)S(1)}, f32[32,32,128]{2,1,0:T(8,128)}, u32[]{:S(2)}) copy-start(f32[32,32,128]{2,1,0:T(8,128)} %param.31) | copy-start | bytes 1572868
  7.2 13.6 %copy-start.22 = (s32[1,16,3]{1,0,2:T(1,128)S(1)}, s32[1,16,3]{1,0,2:T(1,128)}, u32[]{:S(2)}) copy-start(s32[1,16,3]{1,0,2:T(1,128)} %param.32) | copy-start | bytes 580
  7.2 13.6 %copy-start.23 = (f32[1,3,16]{2,0,1:T(1,128)S(1)}, f32[1,3,16]{2,0,1:T(1,128)}, u32[]{:S(2)}) copy-start(f32[1,3,16]{2,0,1:T(1,128)} %param.33) | copy-start | bytes 580
  7.2 13.6 %copy-start.18 = (f32[1,3,4096]{2,0,1:T(1,128)S(1)}, f32[1,3,4096]{2,0,1:T(1,128)}, u32[]{:S(2)}) copy-start(f32[1,3,4096]{2,0,1:T(1,128)} %param.35) | copy-start | bytes 147460
  7.2 14.3 %copy-start.17 = (s32[1,4096,3]{1,0,2:T(1,128)S(1)}, s32[1,4096,3]{1,0,2:T(1,128)}, u32[]{:S(2)}) copy-start(s32[1,4096,3]{1,0,2:T(1,128)} %param.34) | copy-start | bytes 147460
  7.2 248.0 %all-reduce.5.cloned.1.call-start = ((), (), s32[]{:S(2)}) async-start(), calls=%async_computation | async-start | bytes 1048576 | tf_op jit(solution)/shard_map/psum | solution.py:121
  9.5 51.0 %copy-start = (f32[2,32,32,128]{3,2,1,0:T(8,128)}, f32[2,32,32,128]{3,2,1,0:T(8,128)S(1)}, u32[]{:S(2)}) copy-start(f32[2,32,32,128]{3,2,1,0:T(8,128)S(1)} %constant_dynamic-update-slice_fusion) | copy-start | bytes 3145732
  10.3 37.9 %collective-permute-start = (f32[2,4,32,128]{3,2,1,0:T(8,128)}, f32[2,4,32,128]{3,2,1,0:T(8,128)S(1)}, u32[]{:S(2)}, u32[]{:S(2)}) collective-permute-start(f32[2,4,32,128]{3,2,1,0:T(8,128)} %get-tuple-element.641), channel_id=1, source_target_pairs={{8,0},{16,8},{24,16},{32,24},{40,32},{48,40},{56,48},{64,56},{72,6... | collective-permute-start | bytes 393224 | tf_op jit(solution)/shard_map/ppermute | solution.py:20
  18.0 30.2 %collective-permute-start.1 = (f32[2,4,32,128]{3,2,1,0:T(8,128)}, f32[2,4,32,128]{3,2,1,0:T(8,128)S(1)}, u32[]{:S(2)}, u32[]{:S(2)}) collective-permute-start(f32[2,4,32,128]{3,2,1,0:T(8,128)} %get-tuple-element.640), channel_id=1, source_target_pairs={{0,8},{8,16},{16,24},{24,32},{32,40},{40,48},{48,56},{56,64},{64,7... | collective-permute-start | bytes 393224 | tf_op jit(solution)/shard_map/ppermute | solution.py:17
  48.2 6.4 %collective-permute-start.2 = (f32[2,40,4,128]{3,2,1,0:T(4,128)S(1)}, f32[2,40,4,128]{3,2,1,0:T(4,128)S(1)}, u32[]{:S(2)}, u32[]{:S(2)}) collective-permute-start(f32[2,40,4,128]{3,2,1,0:T(4,128)S(1)} %get-tuple-element.635), channel_id=1, source_target_pairs={{1,0},{2,1},{3,2},{4,3},{5,4},{6,5},{7,6},{9,8},{10,9},{11,10},{12... | collective-permute-start | bytes 491528 | tf_op jit(solution)/shard_map/ppermute | solution.py:20
  49.5 5.1 %collective-permute-start.3 = (f32[2,40,4,128]{3,2,1,0:T(4,128)S(1)}, f32[2,40,4,128]{3,2,1,0:T(4,128)S(1)}, u32[]{:S(2)}, u32[]{:S(2)}) collective-permute-start(f32[2,40,4,128]{3,2,1,0:T(4,128)S(1)} %get-tuple-element.634), channel_id=1, source_target_pairs={{0,1},{1,2},{2,3},{3,4},{4,5},{5,6},{6,7},{8,9},{9,10},{10,11},{11... | collective-permute-start | bytes 491528 | tf_op jit(solution)/shard_map/ppermute | solution.py:17
  54.6 0.7 copy-start.14
  55.2 0.7 copy-start.15
  57.4 3.1 %copy-start.6 = (f32[32,32,128]{2,1,0:T(8,128)S(1)}, f32[32,32,128]{2,1,0:T(8,128)}, u32[]{:S(2)}) copy-start(f32[32,32,128]{2,1,0:T(8,128)} %mul.262) | copy-start | bytes 1572868
  60.5 6.2 %copy-start.12 = (f32[32,32,16]{1,0,2:T(8,128)S(1)}, f32[32,32,16]{1,0,2:T(8,128)}, u32[]{:S(2)}) copy-start(f32[32,32,16]{1,0,2:T(8,128)} %reshape.680) | copy-start | bytes 196612
  60.5 6.2 %copy-start.19 = (s32[16]{0:T(128)S(1)}, s32[16]{0:T(128)}, u32[]{:S(2)}) copy-start(s32[16]{0:T(128)} %get-tuple-element.645) | copy-start | bytes 196
  66.8 1.0 copy-start.2
  67.5 1.0 copy-start.5
  67.5 6.8 %copy-start.16 = (f32[4096]{0:T(1024)S(1)}, f32[4096]{0:T(1024)}, u32[]{:S(2)}) copy-start(f32[4096]{0:T(1024)} %get-tuple-element.572) | copy-start | bytes 49156
  68.5 7.3 %collective-permute-start.4 = (f32[2,4,32,128]{3,2,1,0:T(8,128)S(1)}, f32[2,4,32,128]{3,2,1,0:T(8,128)S(1)}, u32[]{:S(2)}, u32[]{:S(2)}) collective-permute-start(f32[2,4,32,128]{3,2,1,0:T(8,128)S(1)} %get-tuple-element.639), channel_id=1, source_target_pairs={{8,0},{16,8},{24,16},{32,24},{40,32},{48,40},{56,48},{64,56},{72,6... | collective-permute-start | bytes 393224 | tf_op jit(solution)/shard_map/ppermute | solution.py:20
  72.4 7.0 %collective-permute-start.5 = (f32[2,4,32,128]{3,2,1,0:T(8,128)S(1)}, f32[2,4,32,128]{3,2,1,0:T(8,128)S(1)}, u32[]{:S(2)}, u32[]{:S(2)}) collective-permute-start(f32[2,4,32,128]{3,2,1,0:T(8,128)S(1)} %get-tuple-element.638), channel_id=1, source_target_pairs={{0,8},{8,16},{16,24},{24,32},{32,40},{40,48},{48,56},{56,64},{64,7... | collective-permute-start | bytes 393224 | tf_op jit(solution)/shard_map/ppermute | solution.py:17
  80.2 32.6 %collective-permute-start.6 = (f32[2,40,4,128]{3,2,1,0:T(4,128)}, f32[2,40,4,128]{3,2,1,0:T(4,128)}, u32[]{:S(2)}, u32[]{:S(2)}) collective-permute-start(f32[2,40,4,128]{3,2,1,0:T(4,128)} %get-tuple-element.631), channel_id=1, source_target_pairs={{1,0},{2,1},{3,2},{4,3},{5,4},{6,5},{7,6},{9,8},{10,9},{11,10},{12... | collective-permute-start | bytes 491528 | tf_op jit(solution)/shard_map/ppermute | solution.py:20
  81.5 31.3 %collective-permute-start.7 = (f32[2,40,4,128]{3,2,1,0:T(4,128)}, f32[2,40,4,128]{3,2,1,0:T(4,128)}, u32[]{:S(2)}, u32[]{:S(2)}) collective-permute-start(f32[2,40,4,128]{3,2,1,0:T(4,128)} %get-tuple-element.630), channel_id=1, source_target_pairs={{0,1},{1,2},{2,3},{3,4},{4,5},{5,6},{6,7},{8,9},{9,10},{10,11},{11... | collective-permute-start | bytes 491528 | tf_op jit(solution)/shard_map/ppermute | solution.py:17
  115.3 3.2 %copy-start.1 = (f32[2,32,32,128]{3,2,1,0:T(8,128)S(1)}, f32[2,32,32,128]{3,2,1,0:T(8,128)}, u32[]{:S(2)}) copy-start(f32[2,32,32,128]{3,2,1,0:T(8,128)} %copy-done) | copy-start | bytes 3145732
  115.3 3.2 %copy-start.7 = (f32[32,32,128]{2,1,0:T(8,128)S(1)}, f32[32,32,128]{2,1,0:T(8,128)}, u32[]{:S(2)}) copy-start(f32[32,32,128]{2,1,0:T(8,128)} %mul.262) | copy-start | bytes 1572868
  118.5 6.3 %copy-start.13 = (f32[32,32,16]{1,0,2:T(8,128)S(1)}, f32[32,32,16]{1,0,2:T(8,128)}, u32[]{:S(2)}) copy-start(f32[32,32,16]{1,0,2:T(8,128)} %reshape.682) | copy-start | bytes 196612
  118.5 6.3 %copy-start.20 = (s32[16]{0:T(128)S(1)}, s32[16]{0:T(128)}, u32[]{:S(2)}) copy-start(s32[16]{0:T(128)} %get-tuple-element.645) | copy-start | bytes 196
  124.8 3.8 %copy-start.4 = (f32[1024,128]{1,0:T(8,128)S(1)}, f32[1024,128]{1,0:T(8,128)}, u32[]{:S(2)}) copy-start(f32[1024,128]{1,0:T(8,128)} %get-tuple-element.415) | copy-start | bytes 1572868
  128.8 7.5 %collective-permute-start.8 = (f32[2,4,32,128]{3,2,1,0:T(8,128)S(1)}, f32[2,4,32,128]{3,2,1,0:T(8,128)S(1)}, u32[]{:S(2)}, u32[]{:S(2)}) collective-permute-start(f32[2,4,32,128]{3,2,1,0:T(8,128)S(1)} %get-tuple-element.637), channel_id=1, source_target_pairs={{8,0},{16,8},{24,16},{32,24},{40,32},{48,40},{56,48},{64,56},{72,6... | collective-permute-start | bytes 393224 | tf_op jit(solution)/shard_map/ppermute | solution.py:20
  130.7 8.2 %collective-permute-start.9 = (f32[2,4,32,128]{3,2,1,0:T(8,128)S(1)}, f32[2,4,32,128]{3,2,1,0:T(8,128)S(1)}, u32[]{:S(2)}, u32[]{:S(2)}) collective-permute-start(f32[2,4,32,128]{3,2,1,0:T(8,128)S(1)} %get-tuple-element.636), channel_id=1, source_target_pairs={{0,8},{8,16},{16,24},{24,32},{32,40},{40,48},{48,56},{56,64},{64,7... | collective-permute-start | bytes 393224 | tf_op jit(solution)/shard_map/ppermute | solution.py:17
  139.7 5.0 %collective-permute-start.10 = (f32[2,40,4,128]{3,2,1,0:T(4,128)}, f32[2,40,4,128]{3,2,1,0:T(4,128)}, u32[]{:S(2)}, u32[]{:S(2)}) collective-permute-start(f32[2,40,4,128]{3,2,1,0:T(4,128)} %get-tuple-element.627), channel_id=1, source_target_pairs={{1,0},{2,1},{3,2},{4,3},{5,4},{6,5},{7,6},{9,8},{10,9},{11,10},{12... | collective-permute-start | bytes 491528 | tf_op jit(solution)/shard_map/ppermute | solution.py:20
  141.0 4.4 %collective-permute-start.11 = (f32[2,40,4,128]{3,2,1,0:T(4,128)}, f32[2,40,4,128]{3,2,1,0:T(4,128)}, u32[]{:S(2)}, u32[]{:S(2)}) collective-permute-start(f32[2,40,4,128]{3,2,1,0:T(4,128)} %get-tuple-element.626), channel_id=1, source_target_pairs={{0,1},{1,2},{2,3},{3,4},{4,5},{5,6},{6,7},{8,9},{9,10},{10,11},{11... | collective-permute-start | bytes 491528 | tf_op jit(solution)/shard_map/ppermute | solution.py:17
  148.3 3.1 %copy-start.8 = (f32[32,32,128]{2,1,0:T(8,128)S(1)}, f32[32,32,128]{2,1,0:T(8,128)}, u32[]{:S(2)}) copy-start(f32[32,32,128]{2,1,0:T(8,128)} %mul.262) | copy-start | bytes 1572868
  151.5 7.4 %copy-start.3 = (f32[1024,128]{1,0:T(8,128)S(1)}, f32[1024,128]{1,0:T(8,128)}, u32[]{:S(2)}) copy-start(f32[1024,128]{1,0:T(8,128)} %get-tuple-element.414) | copy-start | bytes 1572868
  162.3 14.0 %copy-start.11 = (f32[16,32,32]{2,1,0:T(8,128)S(1)}, f32[16,32,32]{2,1,0:T(8,128)}, u32[]{:S(2)}) copy-start(f32[16,32,32]{2,1,0:T(8,128)} %get-tuple-element.642) | copy-start | bytes 196612
  162.3 14.3 %copy-start.21 = (s32[16]{0:T(128)S(1)}, s32[16]{0:T(128)}, u32[]{:S(2)}) copy-start(s32[16]{0:T(128)} %get-tuple-element.645) | copy-start | bytes 196
  176.3 2.8 %copy-start.10 = (f32[2,32,32,128]{3,2,1,0:T(8,128)S(1)}, f32[2,32,32,128]{3,2,1,0:T(8,128)}, u32[]{:S(2)}) copy-start(f32[2,32,32,128]{3,2,1,0:T(8,128)} %get-tuple-element.609) | copy-start | bytes 3145732
Sparse Core Ops, SparseCore 0:
  162.4 92.7 all-reduce.4
where the time goes:
time: 265 us; the launch traced here: 264 us
  waiting for transfers between devices  85.3 us (32%)
  matrix products  62.9 us (24%)
  other arithmetic  53.8 us (20%)
  starting transfers between devices  35.6 us (13%)
  between operations  14.5 us (5%)
  local copies, waits for them, and re-layouts  10.7 us (4%)
    psum x1, waiting for transfers between devices, shards(): gradient = lax.psum(summed, 'shot')  75.2 us
    dot_general x27, matrix products, one_block(): lax.dot_general(plane, hit_z, (((0,), (0,)), ((), ())), precision=lax.Pre...  62.9 us
    add x3, other arithmetic, shards(): earlier = 2.0 * current - later + squared * curved  19.9 us
    ppermute x6, starting transfers between devices, extended_2(): lax.ppermute(lax.slice_in_dim(block, block.shape[dim] - width, None, axis...  18.2 us
    concatenate x9, other arithmetic, extended_2(): block = jnp.concatenate([low, block, high], axis=dim)  17.9 us
    ppermute x6, starting transfers between devices, extended_2(): lax.ppermute(lax.slice_in_dim(block, 0, width, axis=dim), axis, backward)  17.4 us
    mul x25, other arithmetic, one_block(): hit_x[:, :, None] * hit_y[:, None, :]  7.21 us
    ppermute x6, waiting for transfers between devices, extended_2(): lax.ppermute(lax.slice_in_dim(block, block.shape[dim] - width, None, axis...  7.05 us
  transfers between devices with their start and end apart: 13, of which 6 were waited for; matrix products, arithmetic and copies ran while one was open for 28% of the time, Pallas kernels for 0%

commit v1 on v0

--- a/solution.py
+++ b/solution.py
@@ -118,7 +118,7 @@
         earlier = inject(earlier, 1, receivers, misfit[step], anchor_x, anchor_y)
         later = current
         current = earlier
-    gradient = lax.psum(summed, "shot")
+    gradient = jnp.sum(lax.all_gather(summed, "shot"), axis=0)
     return (current[0:1], current[1:2], GRAD_SCALE * gradient)
 
 

time: 265 us -> 247 us (0.932)
  the two profiles are of different devices: /device:TPU:8 before, /device:TPU:1 now
where the time goes in v1:
time: 247 us; the launch traced here: 245 us
  matrix products  62.9 us (25%)
  waiting for transfers between devices  61 us (25%)
  other arithmetic  54.6 us (22%)
  starting transfers between devices  40.8 us (17%)
  between operations  14.5 us (6%)
  local copies, waits for them, and re-layouts  10.5 us (4%)
    dot_general x27, matrix products, one_block(): lax.dot_general(plane, hit_z, (((0,), (0,)), ((), ())), precision=lax.Pre...  62.9 us
    all_gather x1, waiting for transfers between devices, shards(): gradient = jnp.sum(lax.all_gather(summed, 'shot'), axis=0)  53.2 us
    ppermute x6, starting transfers between devices, extended_2(): lax.ppermute(lax.slice_in_dim(block, block.shape[dim] - width, None, axis...  22.2 us
    add x3, other arithmetic, shards(): earlier = 2.0 * current - later + squared * curved  19.9 us
    ppermute x6, starting transfers between devices, extended_2(): lax.ppermute(lax.slice_in_dim(block, 0, width, axis=dim), axis, backward)  18.5 us
    concatenate x9, other arithmetic, extended_2(): block = jnp.concatenate([low, block, high], axis=dim)  17.9 us
    mul x25, other arithmetic, one_block(): hit_x[:, :, None] * hit_y[:, None, :]  7.21 us
  transfers between devices with their start and end apart: 13, of which 8 were waited for; matrix products, arithmetic and copies ran while one was open for 30% of the time, Pallas kernels for 0%

profile of v1, /device:TPU:1, one launch (start us, length us, event | category | flops | bytes accessed | tf_op | source)
XLA Modules:
  0.0 245.4 jit_solution(16877680357560390636)
XLA Ops:
  11.6 4.7 %collective-permute-start.1 = (f32[2,4,32,128]{3,2,1,0:T(8,128)}, f32[2,4,32,128]{3,2,1,0:T(8,128)S(1)}, u32[]{:S(2)}, u32[]{:S(2)}) collective-permute-start(f32[2,4,32,128]{3,2,1,0:T(8,128)} %get-tuple-element.658), channel_id=1, source_target_pairs={{0,8},{8,16},{16,24},{24,32},{32,40},{40,48},{48,56},{56,64},{64,7... | collective-permute-start | bytes 393224 | tf_op jit(solution)/shard_map/ppermute | solution.py:17
  18.6 25.7 %while.60 = (s32[]{:T(128)}, f32[1024,128]{1,0:T(8,128)}, s32[8,512,3]{1,2,0:T(4,128)S(1)}, s32[]{:T(128)}, f32[8,512]{1,0:T(8,128)S(1)}, /*index=5*/s32[]{:T(128)}, s32[]{:T(128)}, s32[]{:T(128)}) while((s32[]{:T(128)}, f32[1024,128]{1,0:T(8,128)}, s32[8,512,3]{1,2,0:T(4,128)S(1)}, s32[]{:T(128)}, ...), condition=%wide.region_1.2_spmd.clone.clone, body=%wide.region_0.1_spmd.clone.clone.sunk | while | flops 806224896 | bytes 5541999 | solution.py:80
  18.9 2.0 convolution_add_fusion.6
  21.2 3.0 %convolution_add_fusion.6 = f32[1024,128]{1,0:T(8,128)} fusion(f32[512,1024]{0,1:T(8,128)S(1)} %bitcast.148, f32[1024,128]{1,0:T(8,128)} %get-tuple-element.810, pred[]{:T(512)S(6)} %compare.91, s32[512]{0:T(512)S(1)} %bitcast.161), kind=kOutput, calls=%fused_computation.6.clone.1 | convolution fusion | flops 805634048 | bytes 3147777 | tf_op jit(solution)/shard_map/while/body/eval_jaxpr/dot_general | solution.py:70
  24.6 3.0 %convolution_add_fusion.6 = f32[1024,128]{1,0:T(8,128)} fusion(f32[512,1024]{0,1:T(8,128)S(1)} %bitcast.148, f32[1024,128]{1,0:T(8,128)} %get-tuple-element.810, pred[]{:T(512)S(6)} %compare.91, s32[512]{0:T(512)S(1)} %bitcast.161), kind=kOutput, calls=%fused_computation.6.clone.1 | convolution fusion | flops 805634048 | bytes 3147777 | tf_op jit(solution)/shard_map/while/body/eval_jaxpr/dot_general | solution.py:70
  27.9 3.0 %convolution_add_fusion.6 = f32[1024,128]{1,0:T(8,128)} fusion(f32[512,1024]{0,1:T(8,128)S(1)} %bitcast.148, f32[1024,128]{1,0:T(8,128)} %get-tuple-element.810, pred[]{:T(512)S(6)} %compare.91, s32[512]{0:T(512)S(1)} %bitcast.161), kind=kOutput, calls=%fused_computation.6.clone.1 | convolution fusion | flops 805634048 | bytes 3147777 | tf_op jit(solution)/shard_map/while/body/eval_jaxpr/dot_general | solution.py:70
  31.3 3.0 %convolution_add_fusion.6 = f32[1024,128]{1,0:T(8,128)} fusion(f32[512,1024]{0,1:T(8,128)S(1)} %bitcast.148, f32[1024,128]{1,0:T(8,128)} %get-tuple-element.810, pred[]{:T(512)S(6)} %compare.91, s32[512]{0:T(512)S(1)} %bitcast.161), kind=kOutput, calls=%fused_computation.6.clone.1 | convolution fusion | flops 805634048 | bytes 3147777 | tf_op jit(solution)/shard_map/while/body/eval_jaxpr/dot_general | solution.py:70
  34.6 3.0 %convolution_add_fusion.6 = f32[1024,128]{1,0:T(8,128)} fusion(f32[512,1024]{0,1:T(8,128)S(1)} %bitcast.148, f32[1024,128]{1,0:T(8,128)} %get-tuple-element.810, pred[]{:T(512)S(6)} %compare.91, s32[512]{0:T(512)S(1)} %bitcast.161), kind=kOutput, calls=%fused_computation.6.clone.1 | convolution fusion | flops 805634048 | bytes 3147777 | tf_op jit(solution)/shard_map/while/body/eval_jaxpr/dot_general | solution.py:70
  37.9 3.0 %convolution_add_fusion.6 = f32[1024,128]{1,0:T(8,128)} fusion(f32[512,1024]{0,1:T(8,128)S(1)} %bitcast.148, f32[1024,128]{1,0:T(8,128)} %get-tuple-element.810, pred[]{:T(512)S(6)} %compare.91, s32[512]{0:T(512)S(1)} %bitcast.161), kind=kOutput, calls=%fused_computation.6.clone.1 | convolution fusion | flops 805634048 | bytes 3147777 | tf_op jit(solution)/shard_map/while/body/eval_jaxpr/dot_general | solution.py:70
  41.3 3.0 %convolution_add_fusion.6 = f32[1024,128]{1,0:T(8,128)} fusion(f32[512,1024]{0,1:T(8,128)S(1)} %bitcast.148, f32[1024,128]{1,0:T(8,128)} %get-tuple-element.810, pred[]{:T(512)S(6)} %compare.91, s32[512]{0:T(512)S(1)} %bitcast.161), kind=kOutput, calls=%fused_computation.6.clone.1 | convolution fusion | flops 805634048 | bytes 3147777 | tf_op jit(solution)/shard_map/while/body/eval_jaxpr/dot_general | solution.py:70
  44.5 8.6 %collective-permute-start.2 = (f32[2,40,4,128]{3,2,1,0:T(4,128)S(1)}, f32[2,40,4,128]{3,2,1,0:T(4,128)S(1)}, u32[]{:S(2)}, u32[]{:S(2)}) collective-permute-start(f32[2,40,4,128]{3,2,1,0:T(4,128)S(1)} %get-tuple-element.653), channel_id=1, source_target_pairs={{1,0},{2,1},{3,2},{4,3},{5,4},{6,5},{7,6},{9,8},{10,9},{11,10},{12... | collective-permute-start | bytes 491528 | tf_op jit(solution)/shard_map/ppermute | solution.py:20
  53.2 1.9 collective-permute-start.3
  58.4 1.5 pad_maximum_fusion
  59.9 3.1 %select_maximum_fusion.8 = f32[2,40,40,136]{3,2,1,0:T(8,128)S(1)} fusion(f32[2,40,4,128]{3,2,1,0:T(4,128)} %copy-done.14, f32[2,40,4,128]{3,2,1,0:T(4,128)} %copy-done.15, f32[2,4,32,128]{3,2,1,0:T(8,128)S(1)} %collective-permute-done, f32[2,32,32,128]{3,2,1,0:T(8,128)S(1)} %constant_dynamic-update-slice_fusion, f32[2,4,32,128]{3,2,1,0:T(8,128)S(1)} %collective-permute-done.1), kind=kLoop, calls=%fused_computation.52 | loop fusion | flops 5222400 | bytes 3379200 | tf_op jit(solution)/shard_map/concatenate | solution.py:21
  63.1 6.2 %fusion.105 = (f32[2,32,32,128]{3,2,1,0:T(8,128)S(1)}, f32[2,32,32,128]{3,2,1,0:T(8,128)}) fusion(f32[1,32,32,128]{3,2,1,0:T(8,128)} %param.30, f32[1,32,32,128]{3,2,1,0:T(8,128)} %param.28, f32[2,32,32,128]{3,2,1,0:T(8,128)S(1)} %constant_dynamic-update-slice_fusion, f32[32,32,128]{2,1,0:T(8,128)S(1)} %copy-done.6, ...), kind=kLoop, calls=%fused_computation.216 | loop fusion | flops 11010048 | bytes 21757952 | tf_op jit(solution)/shard_map/add | solution.py:116
  72.3 4.0 %collective-permute-start.5 = (f32[2,4,32,128]{3,2,1,0:T(8,128)S(1)}, f32[2,4,32,128]{3,2,1,0:T(8,128)S(1)}, u32[]{:S(2)}, u32[]{:S(2)}) collective-permute-start(f32[2,4,32,128]{3,2,1,0:T(8,128)S(1)} %get-tuple-element.656), channel_id=1, source_target_pairs={{0,8},{8,16},{16,24},{24,32},{32,40},{40,48},{48,56},{56,64},{64,7... | collective-permute-start | bytes 393224 | tf_op jit(solution)/shard_map/ppermute | solution.py:17
  79.0 3.7 %collective-permute-start.6 = (f32[2,40,4,128]{3,2,1,0:T(4,128)}, f32[2,40,4,128]{3,2,1,0:T(4,128)}, u32[]{:S(2)}, u32[]{:S(2)}) collective-permute-start(f32[2,40,4,128]{3,2,1,0:T(4,128)} %get-tuple-element.649), channel_id=1, source_target_pairs={{1,0},{2,1},{3,2},{4,3},{5,4},{6,5},{7,6},{9,8},{10,9},{11,10},{12... | collective-permute-start | bytes 491528 | tf_op jit(solution)/shard_map/ppermute | solution.py:20
  82.7 3.5 %collective-permute-start.7 = (f32[2,40,4,128]{3,2,1,0:T(4,128)}, f32[2,40,4,128]{3,2,1,0:T(4,128)}, u32[]{:S(2)}, u32[]{:S(2)}) collective-permute-start(f32[2,40,4,128]{3,2,1,0:T(4,128)} %get-tuple-element.648), channel_id=1, source_target_pairs={{0,1},{1,2},{2,3},{3,4},{4,5},{5,6},{6,7},{8,9},{9,10},{10,11},{11... | collective-permute-start | bytes 491528 | tf_op jit(solution)/shard_map/ppermute | solution.py:17
  86.2 25.7 %while.61 = (s32[]{:T(128)}, f32[1024,128]{1,0:T(8,128)}, s32[8,512,3]{1,2,0:T(4,128)S(1)}, s32[]{:T(128)}, f32[8,512]{1,0:T(8,128)S(1)}, /*index=5*/s32[]{:T(128)}, s32[]{:T(128)}, s32[]{:T(128)}) while((s32[]{:T(128)}, f32[1024,128]{1,0:T(8,128)}, s32[8,512,3]{1,2,0:T(4,128)S(1)}, s32[]{:T(128)}, ...), condition=%wide.region_3.4_spmd.clone.clone, body=%wide.region_2.3_spmd.clone.clone.sunk | while | flops 806224896 | bytes 5541999 | solution.py:80
  86.6 2.0 convolution_add_fusion.7
  88.9 3.0 %convolution_add_fusion.7 = f32[1024,128]{1,0:T(8,128)} fusion(f32[512,1024]{0,1:T(8,128)S(1)} %bitcast.149, f32[1024,128]{1,0:T(8,128)} %get-tuple-element.834, pred[]{:T(512)S(6)} %compare.92, s32[512]{0:T(512)S(1)} %bitcast.162), kind=kOutput, calls=%fused_computation.18.clone.1 | convolution fusion | flops 805634048 | bytes 3147777 | tf_op jit(solution)/shard_map/while/body/eval_jaxpr/dot_general | solution.py:70
  92.2 3.0 %convolution_add_fusion.7 = f32[1024,128]{1,0:T(8,128)} fusion(f32[512,1024]{0,1:T(8,128)S(1)} %bitcast.149, f32[1024,128]{1,0:T(8,128)} %get-tuple-element.834, pred[]{:T(512)S(6)} %compare.92, s32[512]{0:T(512)S(1)} %bitcast.162), kind=kOutput, calls=%fused_computation.18.clone.1 | convolution fusion | flops 805634048 | bytes 3147777 | tf_op jit(solution)/shard_map/while/body/eval_jaxpr/dot_general | solution.py:70
  95.6 3.0 %convolution_add_fusion.7 = f32[1024,128]{1,0:T(8,128)} fusion(f32[512,1024]{0,1:T(8,128)S(1)} %bitcast.149, f32[1024,128]{1,0:T(8,128)} %get-tuple-element.834, pred[]{:T(512)S(6)} %compare.92, s32[512]{0:T(512)S(1)} %bitcast.162), kind=kOutput, calls=%fused_computation.18.clone.1 | convolution fusion | flops 805634048 | bytes 3147777 | tf_op jit(solution)/shard_map/while/body/eval_jaxpr/dot_general | solution.py:70
  98.9 3.0 %convolution_add_fusion.7 = f32[1024,128]{1,0:T(8,128)} fusion(f32[512,1024]{0,1:T(8,128)S(1)} %bitcast.149, f32[1024,128]{1,0:T(8,128)} %get-tuple-element.834, pred[]{:T(512)S(6)} %compare.92, s32[512]{0:T(512)S(1)} %bitcast.162), kind=kOutput, calls=%fused_computation.18.clone.1 | convolution fusion | flops 805634048 | bytes 3147777 | tf_op jit(solution)/shard_map/while/body/eval_jaxpr/dot_general | solution.py:70
  102.3 3.0 %convolution_add_fusion.7 = f32[1024,128]{1,0:T(8,128)} fusion(f32[512,1024]{0,1:T(8,128)S(1)} %bitcast.149, f32[1024,128]{1,0:T(8,128)} %get-tuple-element.834, pred[]{:T(512)S(6)} %compare.92, s32[512]{0:T(512)S(1)} %bitcast.162), kind=kOutput, calls=%fused_computation.18.clone.1 | convolution fusion | flops 805634048 | bytes 3147777 | tf_op jit(solution)/shard_map/while/body/eval_jaxpr/dot_general | solution.py:70
  105.6 3.0 %convolution_add_fusion.7 = f32[1024,128]{1,0:T(8,128)} fusion(f32[512,1024]{0,1:T(8,128)S(1)} %bitcast.149, f32[1024,128]{1,0:T(8,128)} %get-tuple-element.834, pred[]{:T(512)S(6)} %compare.92, s32[512]{0:T(512)S(1)} %bitcast.162), kind=kOutput, calls=%fused_computation.18.clone.1 | convolution fusion | flops 805634048 | bytes 3147777 | tf_op jit(solution)/shard_map/while/body/eval_jaxpr/dot_general | solution.py:70
  109.0 3.0 %convolution_add_fusion.7 = f32[1024,128]{1,0:T(8,128)} fusion(f32[512,1024]{0,1:T(8,128)S(1)} %bitcast.149, f32[1024,128]{1,0:T(8,128)} %get-tuple-element.834, pred[]{:T(512)S(6)} %compare.92, s32[512]{0:T(512)S(1)} %bitcast.162), kind=kOutput, calls=%fused_computation.18.clone.1 | convolution fusion | flops 805634048 | bytes 3147777 | tf_op jit(solution)/shard_map/while/body/eval_jaxpr/dot_general | solution.py:70
  113.9 2.5 %pad_maximum_fusion.1 = (f32[2,40,36,128]{3,2,1,0:T(8,128)S(1)}, f32[2,40,36,128]{3,2,1,0:T(8,128)}) fusion(f32[2,40,4,128]{3,2,1,0:T(4,128)} %collective-permute-done.6, f32[2,4,32,128]{3,2,1,0:T(8,128)S(1)} %collective-permute-done.4, f32[2,32,32,128]{3,2,1,0:T(8,128)S(1)} %fusion.114, f32[2,4,32,128]{3,2,1,0:T(8,128)S(1)} %collective-permute-done.5, ...), kind=kLoop, calls=%fused_computation.77 | loop fusion | flops 2211840 | bytes 4587520 | tf_op jit(solution)/shard_map/concatenate | solution.py:21
  116.4 3.2 %select_maximum_fusion.4 = f32[2,40,40,136]{3,2,1,0:T(8,128)S(1)} fusion(f32[2,40,4,128]{3,2,1,0:T(4,128)} %collective-permute-done.6, f32[2,40,4,128]{3,2,1,0:T(4,128)} %collective-permute-done.7, f32[2,4,32,128]{3,2,1,0:T(8,128)S(1)} %collective-permute-done.4, f32[2,32,32,128]{3,2,1,0:T(8,128)S(1)} %fusion.114, ...), kind=kLoop, calls=%fused_computation.48 | loop fusion | flops 5222400 | bytes 3379200 | tf_op jit(solution)/shard_map/concatenate | solution.py:21
  119.6 6.3 %multiply_add_fusion.1 = (f32[2,32,32,128]{3,2,1,0:T(8,128)}, f32[2,32,32,128]{3,2,1,0:T(8,128)}) fusion(f32[2,32,32,128]{3,2,1,0:T(8,128)S(1)} %copy-done.1, f32[2,32,32,128]{3,2,1,0:T(8,128)S(1)} %fusion.114, f32[32,32,128]{2,1,0:T(8,128)S(1)} %copy-done.7, f32[2,40,40,136]{3,2,1,0:T(8,128)S(1)} %select_maximum_fusion.4, ...), kind=kLoop, calls=%fused_computation.218 | loop fusion | flops 10747904 | bytes 21757952 | tf_op jit(solution)/shard_map/add | solution.py:116
  125.9 2.6 %fusion.25 = f32[2,32,32,128]{3,2,1,0:T(8,128)} fusion(f32[2,32,32,128]{3,2,1,0:T(8,128)} %get-tuple-element.629, f32[32,32,16]{1,0,2:T(8,128)S(1)} %copy-done.13, s32[16]{0:T(128)S(1)} %copy-done.20), kind=kOutput, calls=%fused_computation.87 | convolution fusion | flops 25298944 | bytes 1114176 | tf_op jit(solution)/shard_map/while/body/eval_jaxpr/dot_general | solution.py:70
  131.1 4.7 %collective-permute-start.9 = (f32[2,4,32,128]{3,2,1,0:T(8,128)S(1)}, f32[2,4,32,128]{3,2,1,0:T(8,128)S(1)}, u32[]{:S(2)}, u32[]{:S(2)}) collective-permute-start(f32[2,4,32,128]{3,2,1,0:T(8,128)S(1)} %get-tuple-element.654), channel_id=1, source_target_pairs={{0,8},{8,16},{16,24},{24,32},{32,40},{40,48},{48,56},{56,64},{64,7... | collective-permute-start | bytes 393224 | tf_op jit(solution)/shard_map/ppermute | solution.py:17
  135.8 1.6 collective-permute-done.8
  137.4 1.7 collective-permute-done.9
  139.9 2.3 collective-permute-start.10
  142.2 3.4 %collective-permute-start.11 = (f32[2,40,4,128]{3,2,1,0:T(4,128)}, f32[2,40,4,128]{3,2,1,0:T(4,128)}, u32[]{:S(2)}, u32[]{:S(2)}) collective-permute-start(f32[2,40,4,128]{3,2,1,0:T(4,128)} %get-tuple-element.644), channel_id=1, source_target_pairs={{0,1},{1,2},{2,3},{3,4},{4,5},{5,6},{6,7},{8,9},{9,10},{10,11},{11... | collective-permute-start | bytes 491528 | tf_op jit(solution)/shard_map/ppermute | solution.py:17
  148.0 2.9 %pad_maximum_fusion.2 = (f32[2,40,36,128]{3,2,1,0:T(8,128)}, f32[2,40,36,128]{3,2,1,0:T(8,128)}) fusion(f32[2,40,4,128]{3,2,1,0:T(4,128)} %collective-permute-done.10, f32[2,4,32,128]{3,2,1,0:T(8,128)S(1)} %collective-permute-done.8, f32[2,32,32,128]{3,2,1,0:T(8,128)S(1)} %fusion.115, f32[2,4,32,128]{3,2,1,0:T(8,128)S(1)} %collective-permute-done.9, ...), kind=kLoop, calls=%fused_computation.79 | loop fusion | flops 2211840 | bytes 4587520 | tf_op jit(solution)/shard_map/concatenate | solution.py:21
  151.0 3.1 %select_maximum_fusion = f32[2,40,40,136]{3,2,1,0:T(8,128)S(1)} fusion(f32[2,40,4,128]{3,2,1,0:T(4,128)} %collective-permute-done.10, f32[2,40,4,128]{3,2,1,0:T(4,128)} %collective-permute-done.11, f32[2,4,32,128]{3,2,1,0:T(8,128)S(1)} %collective-permute-done.8, f32[2,32,32,128]{3,2,1,0:T(8,128)S(1)} %fusion.115, ...), kind=kLoop, calls=%fused_computation.44 | loop fusion | flops 5222400 | bytes 3379200 | tf_op jit(solution)/shard_map/concatenate | solution.py:21
  154.1 7.4 %multiply_add_fusion = (f32[2,32,32,128]{3,2,1,0:T(8,128)}, f32[2,32,32,128]{3,2,1,0:T(8,128)}) fusion(f32[2,32,32,128]{3,2,1,0:T(8,128)S(1)} %fusion.114, f32[2,32,32,128]{3,2,1,0:T(8,128)S(1)} %fusion.115, f32[32,32,128]{2,1,0:T(8,128)S(1)} %copy-done.8, f32[2,40,40,136]{3,2,1,0:T(8,128)S(1)} %select_maximum_fusion, ...), kind=kLoop, calls=%fused_computation.217 | loop fusion | flops 10747904 | bytes 21757952 | tf_op jit(solution)/shard_map/add | solution.py:116
  161.5 3.3 %fusion.107 = f32[32,32,128]{2,1,0:T(8,128)} fusion(f32[2,32,32,128]{3,2,1,0:T(8,128)} %get-tuple-element.628, f32[2,32,32,128]{3,2,1,0:T(8,128)} %get-tuple-element.630, f32[2,32,32,128]{3,2,1,0:T(8,128)} %get-tuple-element.632, f32[1,32,32,128]{3,2,1,0:T(8,128)} %param.29, f32[32,32,128]{2,1,0:T(8,128)} %param.31, f32[1,32,32,128]{3,2,1,0:T(8,128)S(1)} %bitcast.152, ...), kind=kLoop, calls=%fused_computation.221 | loop fusion | flops 1441792 | bytes 5242880 | tf_op jit(solution)/shard_map/add | solution.py:85
  164.9 14.0 %while.62 = (s32[]{:T(128)}, f32[1024,128]{1,0:T(8,128)S(1)}, s32[8,512,3]{1,2,0:T(4,128)S(1)}, s32[]{:T(128)}, f32[8,512]{1,0:T(8,128)S(1)}, /*index=5*/s32[]{:T(128)}, s32[]{:T(128)}, s32[]{:T(128)}) while((s32[]{:T(128)}, f32[1024,128]{1,0:T(8,128)S(1)}, s32[8,512,3]{1,2,0:T(4,128)S(1)}, s32[]{:T(128)}, ...), condition=%wide.region_5.6_spmd.clone.clone, body=%wide.region_4.5_spmd.clone.clone.sunk | while | flops 806224896 | bytes 5541999 | solution.py:80
  165.3 1.4 convolution_add_fusion.8
  167.0 1.4 convolution_add_fusion.8
  174.0 1.4 convolution_add_fusion.8
  175.8 1.4 convolution_add_fusion.8
  179.2 2.5 %fusion.26 = f32[1,32,32,128]{3,2,1,0:T(8,128)} fusion(f32[2,32,32,128]{3,2,1,0:T(8,128)} %get-tuple-element.627, f32[32,32,16]{1,0,2:T(8,128)S(1)} %reshape.684, s32[16]{0:T(128)S(1)} %copy-done.21), kind=kOutput, calls=%fused_computation.88 | convolution fusion | flops 25298944 | bytes 1114176 | tf_op jit(solution)/shard_map/while/body/eval_jaxpr/dot_general | solution.py:70
  182.6 53.2 %all-gather.3.cloned.1.call-done = f32[128,32,128]{2,1,0:T(8,128)} async-done(((f32[32,32,128]{2,1,0:T(8,128)}), f32[128,32,128]{2,1,0:T(8,128)}) %all-gather.3.cloned.1.call-update) | async-done | bytes 2097168 | tf_op jit(solution)/shard_map/all_gather | solution.py:121
  235.9 1.9 reduce_sum.9
  (247 shorter events, 38.2 us)
Async XLA Ops:
  7.2 9.1 %copy-start.9 = (f32[32,32,128]{2,1,0:T(8,128)S(1)}, f32[32,32,128]{2,1,0:T(8,128)}, u32[]{:S(2)}) copy-start(f32[32,32,128]{2,1,0:T(8,128)} %param.31) | copy-start | bytes 1572868
  7.2 9.9 %copy-start.22 = (s32[1,16,3]{1,0,2:T(1,128)S(1)}, s32[1,16,3]{1,0,2:T(1,128)}, u32[]{:S(2)}) copy-start(s32[1,16,3]{1,0,2:T(1,128)} %param.32) | copy-start | bytes 580
  7.2 9.9 %copy-start.23 = (f32[1,3,16]{2,0,1:T(1,128)S(1)}, f32[1,3,16]{2,0,1:T(1,128)}, u32[]{:S(2)}) copy-start(f32[1,3,16]{2,0,1:T(1,128)} %param.33) | copy-start | bytes 580
  7.2 9.9 %copy-start.18 = (f32[1,3,4096]{2,0,1:T(1,128)S(1)}, f32[1,3,4096]{2,0,1:T(1,128)}, u32[]{:S(2)}) copy-start(f32[1,3,4096]{2,0,1:T(1,128)} %param.35) | copy-start | bytes 147460
  7.2 10.7 %copy-start.17 = (s32[1,4096,3]{1,0,2:T(1,128)S(1)}, s32[1,4096,3]{1,0,2:T(1,128)}, u32[]{:S(2)}) copy-start(s32[1,4096,3]{1,0,2:T(1,128)} %param.34) | copy-start | bytes 147460
  7.2 228.6 %all-gather.3.cloned.1.call-start = ((), (), s32[]{:S(2)}) async-start(), calls=%async_computation | async-start | bytes 2621440 | tf_op jit(solution)/shard_map/all_gather | solution.py:121
  9.5 53.6 %copy-start = (f32[2,32,32,128]{3,2,1,0:T(8,128)}, f32[2,32,32,128]{3,2,1,0:T(8,128)S(1)}, u32[]{:S(2)}) copy-start(f32[2,32,32,128]{3,2,1,0:T(8,128)S(1)} %constant_dynamic-update-slice_fusion) | copy-start | bytes 3145732
  10.3 34.2 %collective-permute-start = (f32[2,4,32,128]{3,2,1,0:T(8,128)}, f32[2,4,32,128]{3,2,1,0:T(8,128)S(1)}, u32[]{:S(2)}, u32[]{:S(2)}) collective-permute-start(f32[2,4,32,128]{3,2,1,0:T(8,128)} %get-tuple-element.659), channel_id=1, source_target_pairs={{8,0},{16,8},{24,16},{32,24},{40,32},{48,40},{56,48},{64,56},{72,6... | collective-permute-start | bytes 393224 | tf_op jit(solution)/shard_map/ppermute | solution.py:20
  11.6 32.9 %collective-permute-start.1 = (f32[2,4,32,128]{3,2,1,0:T(8,128)}, f32[2,4,32,128]{3,2,1,0:T(8,128)S(1)}, u32[]{:S(2)}, u32[]{:S(2)}) collective-permute-start(f32[2,4,32,128]{3,2,1,0:T(8,128)} %get-tuple-element.658), channel_id=1, source_target_pairs={{0,8},{8,16},{16,24},{24,32},{32,40},{40,48},{48,56},{56,64},{64,7... | collective-permute-start | bytes 393224 | tf_op jit(solution)/shard_map/ppermute | solution.py:17
  44.5 12.6 %collective-permute-start.2 = (f32[2,40,4,128]{3,2,1,0:T(4,128)S(1)}, f32[2,40,4,128]{3,2,1,0:T(4,128)S(1)}, u32[]{:S(2)}, u32[]{:S(2)}) collective-permute-start(f32[2,40,4,128]{3,2,1,0:T(4,128)S(1)} %get-tuple-element.653), channel_id=1, source_target_pairs={{1,0},{2,1},{3,2},{4,3},{5,4},{6,5},{7,6},{9,8},{10,9},{11,10},{12... | collective-permute-start | bytes 491528 | tf_op jit(solution)/shard_map/ppermute | solution.py:20
  53.2 4.2 %collective-permute-start.3 = (f32[2,40,4,128]{3,2,1,0:T(4,128)S(1)}, f32[2,40,4,128]{3,2,1,0:T(4,128)S(1)}, u32[]{:S(2)}, u32[]{:S(2)}) collective-permute-start(f32[2,40,4,128]{3,2,1,0:T(4,128)S(1)} %get-tuple-element.652), channel_id=1, source_target_pairs={{0,1},{1,2},{2,3},{3,4},{4,5},{5,6},{6,7},{8,9},{9,10},{10,11},{11... | collective-permute-start | bytes 491528 | tf_op jit(solution)/shard_map/ppermute | solution.py:17
  57.1 0.7 copy-start.14
  57.8 0.7 copy-start.15
  59.9 3.1 %copy-start.6 = (f32[32,32,128]{2,1,0:T(8,128)S(1)}, f32[32,32,128]{2,1,0:T(8,128)}, u32[]{:S(2)}) copy-start(f32[32,32,128]{2,1,0:T(8,128)} %mul.262) | copy-start | bytes 1572868
  63.1 6.2 %copy-start.12 = (f32[32,32,16]{1,0,2:T(8,128)S(1)}, f32[32,32,16]{1,0,2:T(8,128)}, u32[]{:S(2)}) copy-start(f32[32,32,16]{1,0,2:T(8,128)} %reshape.680) | copy-start | bytes 196612
  63.1 6.2 %copy-start.19 = (s32[16]{0:T(128)S(1)}, s32[16]{0:T(128)}, u32[]{:S(2)}) copy-start(s32[16]{0:T(128)} %get-tuple-element.663) | copy-start | bytes 196
  69.3 1.0 copy-start.2
  70.0 1.0 copy-start.5
  70.1 6.3 %copy-start.16 = (f32[4096]{0:T(1024)S(1)}, f32[4096]{0:T(1024)}, u32[]{:S(2)}) copy-start(f32[4096]{0:T(1024)} %get-tuple-element.590) | copy-start | bytes 49156
  71.0 6.4 %collective-permute-start.4 = (f32[2,4,32,128]{3,2,1,0:T(8,128)S(1)}, f32[2,4,32,128]{3,2,1,0:T(8,128)S(1)}, u32[]{:S(2)}, u32[]{:S(2)}) collective-permute-start(f32[2,4,32,128]{3,2,1,0:T(8,128)S(1)} %get-tuple-element.657), channel_id=1, source_target_pairs={{8,0},{16,8},{24,16},{32,24},{40,32},{48,40},{56,48},{64,56},{72,6... | collective-permute-start | bytes 393224 | tf_op jit(solution)/shard_map/ppermute | solution.py:20
  72.3 5.9 %collective-permute-start.5 = (f32[2,4,32,128]{3,2,1,0:T(8,128)S(1)}, f32[2,4,32,128]{3,2,1,0:T(8,128)S(1)}, u32[]{:S(2)}, u32[]{:S(2)}) collective-permute-start(f32[2,4,32,128]{3,2,1,0:T(8,128)S(1)} %get-tuple-element.656), channel_id=1, source_target_pairs={{0,8},{8,16},{16,24},{24,32},{32,40},{40,48},{48,56},{56,64},{64,7... | collective-permute-start | bytes 393224 | tf_op jit(solution)/shard_map/ppermute | solution.py:17
  79.0 34.9 %collective-permute-start.6 = (f32[2,40,4,128]{3,2,1,0:T(4,128)}, f32[2,40,4,128]{3,2,1,0:T(4,128)}, u32[]{:S(2)}, u32[]{:S(2)}) collective-permute-start(f32[2,40,4,128]{3,2,1,0:T(4,128)} %get-tuple-element.649), channel_id=1, source_target_pairs={{1,0},{2,1},{3,2},{4,3},{5,4},{6,5},{7,6},{9,8},{10,9},{11,10},{12... | collective-permute-start | bytes 491528 | tf_op jit(solution)/shard_map/ppermute | solution.py:20
  82.7 31.2 %collective-permute-start.7 = (f32[2,40,4,128]{3,2,1,0:T(4,128)}, f32[2,40,4,128]{3,2,1,0:T(4,128)}, u32[]{:S(2)}, u32[]{:S(2)}) collective-permute-start(f32[2,40,4,128]{3,2,1,0:T(4,128)} %get-tuple-element.648), channel_id=1, source_target_pairs={{0,1},{1,2},{2,3},{3,4},{4,5},{5,6},{6,7},{8,9},{9,10},{10,11},{11... | collective-permute-start | bytes 491528 | tf_op jit(solution)/shard_map/ppermute | solution.py:17
  116.3 3.2 %copy-start.1 = (f32[2,32,32,128]{3,2,1,0:T(8,128)S(1)}, f32[2,32,32,128]{3,2,1,0:T(8,128)}, u32[]{:S(2)}) copy-start(f32[2,32,32,128]{3,2,1,0:T(8,128)} %copy-done) | copy-start | bytes 3145732
  116.3 3.2 %copy-start.7 = (f32[32,32,128]{2,1,0:T(8,128)S(1)}, f32[32,32,128]{2,1,0:T(8,128)}, u32[]{:S(2)}) copy-start(f32[32,32,128]{2,1,0:T(8,128)} %mul.262) | copy-start | bytes 1572868
  119.6 6.3 %copy-start.13 = (f32[32,32,16]{1,0,2:T(8,128)S(1)}, f32[32,32,16]{1,0,2:T(8,128)}, u32[]{:S(2)}) copy-start(f32[32,32,16]{1,0,2:T(8,128)} %reshape.682) | copy-start | bytes 196612
  119.6 6.3 %copy-start.20 = (s32[16]{0:T(128)S(1)}, s32[16]{0:T(128)}, u32[]{:S(2)}) copy-start(s32[16]{0:T(128)} %get-tuple-element.663) | copy-start | bytes 196
  125.8 3.8 %copy-start.4 = (f32[1024,128]{1,0:T(8,128)S(1)}, f32[1024,128]{1,0:T(8,128)}, u32[]{:S(2)}) copy-start(f32[1024,128]{1,0:T(8,128)} %get-tuple-element.415) | copy-start | bytes 1572868
  129.8 7.6 %collective-permute-start.8 = (f32[2,4,32,128]{3,2,1,0:T(8,128)S(1)}, f32[2,4,32,128]{3,2,1,0:T(8,128)S(1)}, u32[]{:S(2)}, u32[]{:S(2)}) collective-permute-start(f32[2,4,32,128]{3,2,1,0:T(8,128)S(1)} %get-tuple-element.655), channel_id=1, source_target_pairs={{8,0},{16,8},{24,16},{32,24},{40,32},{48,40},{56,48},{64,56},{72,6... | collective-permute-start | bytes 393224 | tf_op jit(solution)/shard_map/ppermute | solution.py:20
  131.1 8.0 %collective-permute-start.9 = (f32[2,4,32,128]{3,2,1,0:T(8,128)S(1)}, f32[2,4,32,128]{3,2,1,0:T(8,128)S(1)}, u32[]{:S(2)}, u32[]{:S(2)}) collective-permute-start(f32[2,4,32,128]{3,2,1,0:T(8,128)S(1)} %get-tuple-element.654), channel_id=1, source_target_pairs={{0,8},{8,16},{16,24},{24,32},{32,40},{40,48},{48,56},{56,64},{64,7... | collective-permute-start | bytes 393224 | tf_op jit(solution)/shard_map/ppermute | solution.py:17
  139.9 6.9 %collective-permute-start.10 = (f32[2,40,4,128]{3,2,1,0:T(4,128)}, f32[2,40,4,128]{3,2,1,0:T(4,128)}, u32[]{:S(2)}, u32[]{:S(2)}) collective-permute-start(f32[2,40,4,128]{3,2,1,0:T(4,128)} %get-tuple-element.645), channel_id=1, source_target_pairs={{1,0},{2,1},{3,2},{4,3},{5,4},{6,5},{7,6},{9,8},{10,9},{11,10},{12... | collective-permute-start | bytes 491528 | tf_op jit(solution)/shard_map/ppermute | solution.py:20
  142.2 5.8 %collective-permute-start.11 = (f32[2,40,4,128]{3,2,1,0:T(4,128)}, f32[2,40,4,128]{3,2,1,0:T(4,128)}, u32[]{:S(2)}, u32[]{:S(2)}) collective-permute-start(f32[2,40,4,128]{3,2,1,0:T(4,128)} %get-tuple-element.644), channel_id=1, source_target_pairs={{0,1},{1,2},{2,3},{3,4},{4,5},{5,6},{6,7},{8,9},{9,10},{10,11},{11... | collective-permute-start | bytes 491528 | tf_op jit(solution)/shard_map/ppermute | solution.py:17
  151.0 3.1 %copy-start.8 = (f32[32,32,128]{2,1,0:T(8,128)S(1)}, f32[32,32,128]{2,1,0:T(8,128)}, u32[]{:S(2)}) copy-start(f32[32,32,128]{2,1,0:T(8,128)} %mul.262) | copy-start | bytes 1572868
  154.1 7.4 %copy-start.3 = (f32[1024,128]{1,0:T(8,128)S(1)}, f32[1024,128]{1,0:T(8,128)}, u32[]{:S(2)}) copy-start(f32[1024,128]{1,0:T(8,128)} %get-tuple-element.414) | copy-start | bytes 1572868
  164.9 14.0 %copy-start.11 = (f32[16,32,32]{2,1,0:T(8,128)S(1)}, f32[16,32,32]{2,1,0:T(8,128)}, u32[]{:S(2)}) copy-start(f32[16,32,32]{2,1,0:T(8,128)} %get-tuple-element.660) | copy-start | bytes 196612
  164.9 14.3 %copy-start.21 = (s32[16]{0:T(128)S(1)}, s32[16]{0:T(128)}, u32[]{:S(2)}) copy-start(s32[16]{0:T(128)} %get-tuple-element.663) | copy-start | bytes 196
  178.9 2.8 %copy-start.10 = (f32[2,32,32,128]{3,2,1,0:T(8,128)S(1)}, f32[2,32,32,128]{3,2,1,0:T(8,128)}, u32[]{:S(2)}) copy-start(f32[2,32,32,128]{3,2,1,0:T(8,128)} %get-tuple-element.627) | copy-start | bytes 3145732
Sparse Core Ops, SparseCore 0:
  165.0 70.7 all-gather.2
